TPU v7x, 256 devices: a whole 4x4x8 slice. The times are simulated.
256 devices in a mesh: row: 8 (over y_lo, x), col: 16 (over z, core), layer: 2 (over y_hi).
Axes of the slice: x: 4, y: 4 (y_hi: 2, y_lo: 2; y = y_hi * 2 + y_lo), z: 8, core: 2. Of those that a mesh axis runs over, the one named last changes fastest.
Arguments:
- basis_left: bfloat16 [32768, 32, 128], P(('row', 'col', 'layer')), may hold values from -6 to 6
- basis_right: bfloat16 [32768, 32, 128], P(('row', 'col', 'layer')), may hold values from -6 to 6
- grid_weight: float32 [32768, 128], P(('row', 'col', 'layer')), may hold values from -0.3 to 0.3
- task_owner: int32 [32768, 1], P(('row', 'col', 'layer')), may hold values from 0 to 127; in each aligned block of 128 rows (0 to 127, 128 to 255, ...) at most 2 rows name the same one
- task_block: int32 [32768], P(('row', 'col', 'layer')), may hold values from 0 to 511
- core_matrix: float32 [8192, 8192], P('row', 'col'), may hold values from -6 to 6
- block_mask: int32 [256, 256], P('row', 'col'), may hold values 0 or 1
Outputs:
- ks_matrix: float32 [8192, 8192], P('row', ('col', 'layer'))
- density: float32 [8192, 8192], P('row', ('col', 'layer'))
Inputs may be any that keep to these rules, and one draw needn't show every extreme that they name: `task_owner`: in the tasks of one device no owner is named more than 2 times, a bound that some block reaches.
All inputs are finite; a program needn't handle non-finite values. No bound on the sum of `block_mask` on one device may be relied on, other than what follows from the above.
Results may differ from a plain program's by a relative error of at most 0.0053.
Values may be sent and summed in bfloat16 or wider, within the bound.
No kernel may reach another device: no remote copies, remote signals or barrier semaphores. Data moves between devices by JAX's collectives and lax.ppermute only.
A program may use at most 128 MiB of HBM per device.

v0:
```python
import math
import jax
import jax.numpy as jnp
from jax import lax
from jax.sharding import PartitionSpec as P

BS = 32
NBLK = 256
COUPLING = 2.5


def local(basis_left, basis_right, grid_weight, task_owner, task_block, core_matrix, block_mask):
    rows_local, panel_width = core_matrix.shape
    layers = lax.axis_size("layer")
    row_count = lax.axis_size("row")
    col_count = lax.axis_size("col")
    owners = row_count * col_count
    subwidth = panel_width // layers
    matrix_order = NBLK * BS
    block_rows = NBLK // row_count
    block_cols = NBLK // col_count
    owned_blocks = block_rows * block_cols
    task_count = basis_left.shape[0]
    capacity = max(2, 2 * task_count // owners)
    row_index = lax.axis_index("row")
    col_index = lax.axis_index("col")
    layer_index = lax.axis_index("layer")
    weighted = (basis_left * grid_weight[:, None, :]).astype(jnp.bfloat16)
    blocks = jnp.einsum("tag,tbg->tab", weighted, basis_right, preferred_element_type=jnp.float32)
    blocks = blocks.reshape(task_count, BS * BS)
    target = task_owner[:, 0]
    onehot = (target[:, None] == jnp.arange(owners, dtype=jnp.int32)[None, :]).astype(jnp.int32)
    before = jnp.cumsum(onehot, axis=0) - onehot
    slot_index = jnp.sum(before * onehot, axis=1)
    position = target * capacity + slot_index
    outgoing = jnp.zeros((owners * capacity, BS * BS), jnp.float32).at[position].set(blocks)
    labels = (
        jnp.full((owners * capacity,), float(owned_blocks), jnp.float32)
        .at[position]
        .set(task_block.astype(jnp.float32))
    )
    arrived, arrived_ids = (
        lax.all_to_all(
            outgoing.reshape(owners, capacity, BS * BS),
            ("row", "col"),
            split_axis=0,
            concat_axis=0,
            tiled=True,
        ),
        lax.all_to_all(
            labels.reshape(owners, capacity),
            ("row", "col"),
            split_axis=0,
            concat_axis=0,
            tiled=True,
        ),
    )
    collected = (
        jnp.zeros((owned_blocks, BS * BS), jnp.float32)
        .at[arrived_ids.reshape(-1).astype(jnp.int32)]
        .add(arrived.reshape(-1, BS * BS), mode="drop")
    )
    local_panel = (
        collected.reshape(block_rows, block_cols, BS, BS)
        .transpose(0, 2, 1, 3)
        .reshape(rows_local, panel_width)
    )
    block_row_ids = row_index * block_rows + jnp.arange(block_rows, dtype=jnp.int32)
    block_col_ids = col_index * block_cols + jnp.arange(block_cols, dtype=jnp.int32)
    pattern_blocks = (block_mask != 0) | (block_row_ids[:, None] == block_col_ids[None, :])
    pattern = jnp.repeat(jnp.repeat(pattern_blocks.astype(jnp.float32), BS, 0), BS, 1)
    global_row = row_index * rows_local + jnp.arange(rows_local, dtype=jnp.int32)
    global_col = col_index * panel_width + jnp.arange(panel_width, dtype=jnp.int32)
    identity = (global_row[:, None] == global_col[None, :]).astype(jnp.float32)
    coupling_scale = COUPLING / math.sqrt(matrix_order)

    def own_columns(panel):
        return lax.dynamic_index_in_dim(
            panel.reshape(rows_local, layers, subwidth), layer_index, axis=1, keepdims=False
        )

    grid_terms = lax.psum_scatter(local_panel, "layer", scatter_dimension=1, tiled=True)
    ks_out = own_columns(core_matrix) + grid_terms
    pattern_own = own_columns(pattern)
    identity_own = own_columns(identity)
    initial = (pattern_own * (0.5 * identity_own - coupling_scale * ks_out)).astype(jnp.bfloat16)
    column_panel = lax.all_gather(initial, "row", axis=0, tiled=True)

    def accumulate(incoming):
        return jnp.dot(incoming, column_panel, preferred_element_type=jnp.float32)

    square = pattern_own * accumulate(lax.all_gather(initial, ("col", "layer"), axis=1, tiled=True))
    cube_term = pattern_own * accumulate(
        lax.all_gather(square.astype(jnp.bfloat16), ("col", "layer"), axis=1, tiled=True)
    )
    density = 3.0 * square - 2.0 * cube_term
    return (ks_out, density)


def solution(mesh):
    placed = (
        P(("row", "col", "layer"), None, None),
        P(("row", "col", "layer"), None, None),
        P(("row", "col", "layer"), None),
        P(("row", "col", "layer"), None),
        P(("row", "col", "layer")),
        P("row", "col"),
        P("row", "col"),
    )
    return jax.shard_map(
        local,
        mesh=mesh,
        in_specs=placed,
        out_specs=(P("row", ("col", "layer")), P("row", ("col", "layer"))),
        check_vma=False,
    )
```

profile of v0, /device:TPU:1, one launch (start us, length us, event | category | flops | bytes accessed | tf_op | source)
XLA Modules:
  0.0 535.9 jit_solution(16276669535692589134)
XLA Ops:
  10.3 1.0 scatter_custom_fusion
  12.1 14.8 %all-to-all-start = ((f32[128,1,2]{2,1,0:T(1,128)}), f32[128,1,2]{2,1,0:T(1,128)S(1)}, u32[]{:S(2)}, u32[]{:S(2)}) async-start(f32[128,1,2]{2,1,0:T(1,128)} %bitcast.4), calls=%async_computation | async-start | bytes 131072 | tf_op jit(solution)/shard_map/all_to_all | solution.py:50
  26.9 1.9 fusion.2
  28.8 1.3 copy.22
  30.3 1.3 scatter_custom_fusion.1
  31.5 1.6 reshape.84
  33.1 4.3 all-to-all-done
  37.4 8.1 %all-to-all-start.1 = ((f32[128,2,1024]{2,1,0:T(2,128)}), f32[128,2,1024]{2,1,0:T(2,128)S(1)}, u32[]{:S(2)}, u32[]{:S(2)}) async-start(f32[128,2,1024]{2,1,0:T(2,128)} %reshape.84), calls=%async_computation.1 | async-start | bytes 2097152 | tf_op jit(solution)/shard_map/all_to_all | solution.py:43
  46.0 28.4 %all-to-all-done.1 = f32[128,2,1024]{2,1,0:T(2,128)S(1)} async-done(((f32[128,2,1024]{2,1,0:T(2,128)}), f32[128,2,1024]{2,1,0:T(2,128)S(1)}, u32[]{:S(2)}, u32[]{:S(2)}) %all-to-all-start.1) | async-done | bytes 1048608 | tf_op jit(solution)/shard_map/all_to_all | solution.py:43
  74.4 1.7 reshape.109
  76.1 4.0 scatter_custom_fusion.2
  80.1 4.8 reshape.86
  84.8 14.2 %copy.24 = f32[32,32,16,32]{3,2,1,0:T(8,128)} copy(f32[32,32,16,32]{3,1,2,0:T(8,128)} %bitcast.38) | data formatting | bytes 4194304 | tf_op jit(solution)/shard_map/transpose | solution.py:65
  99.0 7.3 %reshape.87 = f32[1024,512]{1,0:T(8,128)} reshape(f32[32,32,16,32]{3,2,1,0:T(8,128)} %copy.24) | data formatting | bytes 4194304 | tf_op jit(solution)/shard_map/reshape | solution.py:66
  107.4 1.3 copy.25
  108.7 2.6 reshape.82
  111.3 0.9 constant_dynamic-slice_fusion.2
  112.2 30.3 %reduce-scatter.2.cloned.1.call-done = f32[1024,256]{1,0:T(8,128)} async-done(((f32[1024,512]{1,0:T(8,128)}), f32[1024,256]{1,0:T(8,128)}) %reduce-scatter.2.cloned.1.call-update) | async-done | bytes 1048592 | tf_op jit(solution)/shard_map/reduce_scatter | solution.py:82
  142.4 3.0 fusion.5
  146.2 53.9 %all-gather.6.cloned.1.call-done = bf16[8192,256]{1,0:T(8,128)(2,1)} async-done(((bf16[1024,256]{1,0:T(8,128)(2,1)}), bf16[8192,256]{1,0:T(8,128)(2,1)}) %all-gather.6.cloned.1.call-update) | async-done | bytes 4194320 | tf_op jit(solution)/shard_map/all_gather | solution.py:87
  200.1 154.9 %all-gather.4.cloned.1.call-done = bf16[1024,8192]{1,0:T(8,128)(2,1)} async-done(((bf16[1024,256]{1,0:T(8,128)(2,1)}), bf16[1024,8192]{1,0:T(8,128)(2,1)}) %all-gather.4.cloned.1.call-update) | async-done | bytes 16777232 | tf_op jit(solution)/shard_map/all_gather | solution.py:92
  355.0 12.5 %fusion.16 = (bf16[1024,256]{1,0:T(8,128)(2,1)}, f32[1024,256]{1,0:T(8,128)S(1)}) fusion(bf16[1024,8192]{1,0:T(8,128)(2,1)} %all-gather.4.cloned.1.call-done, bf16[8192,256]{1,0:T(8,128)(2,1)} %all-gather.6.cloned.1.call-done, f32[1024,1,256]{2,0,1:T(8,128)} %copy.25), kind=kOutput, calls=%fused_computation.37 | convolution fusion | flops 4295491584 | bytes 23592960 | tf_op jit(solution)/shard_map/dot_general | solution.py:90
  367.6 149.2 %all-gather.8.cloned.1.call-done = bf16[1024,8192]{1,0:T(8,128)(2,1)} async-done(((bf16[1024,256]{1,0:T(8,128)(2,1)}), bf16[1024,8192]{1,0:T(8,128)(2,1)}) %all-gather.8.cloned.1.call-update) | async-done | bytes 16777232 | tf_op jit(solution)/shard_map/all_gather | solution.py:94
  516.8 12.5 %fusion.1 = f32[1024,256]{1,0:T(8,128)} fusion(bf16[1024,8192]{1,0:T(8,128)(2,1)} %all-gather.8.cloned.1.call-done, bf16[8192,256]{1,0:T(8,128)(2,1)} %all-gather.6.cloned.1.call-done, f32[1024,1,256]{2,0,1:T(8,128)S(1)} %copy-done.2, f32[1024,256]{1,0:T(8,128)S(1)} %get-tuple-element.5), kind=kOutput, calls=%fused_computation.7 | convolution fusion | flops 4296015872 | bytes 24117248 | tf_op jit(solution)/shard_map/dot_general | solution.py:90
  (36 shorter events, 6.3 us)
Async XLA Ops:
  7.2 19.7 %copy-start = (bf16[128,32,128]{2,1,0:T(8,128)(2,1)S(1)}, bf16[128,32,128]{2,1,0:T(8,128)(2,1)}, u32[]{:S(2)}) copy-start(bf16[128,32,128]{2,1,0:T(8,128)(2,1)} %param.8) | copy-start | bytes 3145732
  12.1 25.4 %all-to-all-start = ((f32[128,1,2]{2,1,0:T(1,128)}), f32[128,1,2]{2,1,0:T(1,128)S(1)}, u32[]{:S(2)}, u32[]{:S(2)}) async-start(f32[128,1,2]{2,1,0:T(1,128)} %bitcast.4), calls=%async_computation | async-start | bytes 131072 | tf_op jit(solution)/shard_map/all_to_all | solution.py:50
  37.4 36.9 %all-to-all-start.1 = ((f32[128,2,1024]{2,1,0:T(2,128)}), f32[128,2,1024]{2,1,0:T(2,128)S(1)}, u32[]{:S(2)}, u32[]{:S(2)}) async-start(f32[128,2,1024]{2,1,0:T(2,128)} %reshape.84), calls=%async_computation.1 | async-start | bytes 2097152 | tf_op jit(solution)/shard_map/all_to_all | solution.py:43
  45.6 96.9 %reduce-scatter.2.cloned.1.call-start = ((), (), s32[]{:S(2)}) async-start(), calls=%async_computation.3 | async-start | bytes 3145728 | tf_op jit(solution)/shard_map/reduce_scatter | solution.py:82
  99.0 7.7 %copy-start.3 = (s32[32,16]{0,1:T(8,128)S(1)}, s32[32,16]{0,1:T(8,128)}, u32[]{:S(2)}) copy-start(s32[32,16]{0,1:T(8,128)} %param.13) | copy-start | bytes 6148
  106.3 93.8 %all-gather.6.cloned.1.call-start = ((), (), s32[]{:S(2)}) async-start(), calls=%async_computation.5 | async-start | bytes 4718592 | tf_op jit(solution)/shard_map/all_gather | solution.py:87
  145.4 209.6 %all-gather.4.cloned.1.call-start = ((), (), s32[]{:S(2)}) async-start(), calls=%async_computation.4 | async-start | bytes 17301504 | tf_op jit(solution)/shard_map/all_gather | solution.py:92
  146.2 370.6 %copy-start.2 = (f32[1024,1,256]{2,0,1:T(8,128)S(1)}, f32[1024,1,256]{2,0,1:T(8,128)}, u32[]{:S(2)}) copy-start(f32[1024,1,256]{2,0,1:T(8,128)} %copy.25) | copy-start | bytes 3145732
  146.2 370.6 %all-gather.8.cloned.1.call-start = ((), (), s32[]{:S(2)}) async-start(), calls=%async_computation.6 | async-start | bytes 17301504 | tf_op jit(solution)/shard_map/all_gather | solution.py:94
  516.8 12.5 %copy-start.1 = (bf16[128,32,128]{2,1,0:T(8,128)(2,1)S(1)}, bf16[128,32,128]{2,1,0:T(8,128)(2,1)}, u32[]{:S(2)}) copy-start(bf16[128,32,128]{2,1,0:T(8,128)(2,1)} %param.8) | copy-start | bytes 3145732
Sparse Core Ops, SparseCore 0:
  106.5 35.9 reduce-scatter.1
  145.6 54.5 all-gather.5
  203.0 151.9 all-gather.3
  367.7 149.0 all-gather.7
where the time goes:
time: 536 us
  waiting for transfers between devices  422 us (79%)
  local copies, waits for them, and re-layouts  39.6 us (7%)
  matrix products  26.9 us (5%)
  starting transfers between devices  23.3 us (4%)
  between operations  14 us (3%)
  other arithmetic  10.4 us (2%)
    all_gather x1, waiting for transfers between devices, local(): lax.all_gather(initial, ('col', 'layer'), axis=1, tiled=True)  155 us
    all_gather x1, waiting for transfers between devices, local(): lax.all_gather(square.astype(jnp.bfloat16), ('col', 'layer'), axis=1, til...  149 us
    all_gather x1, waiting for transfers between devices, local(): column_panel = lax.all_gather(initial, 'row', axis=0, tiled=True)  53.9 us
    reduce_scatter x1, waiting for transfers between devices, local(): lax.psum_scatter(local_panel, 'layer', scatter_dimension=1, tiled=True)  30.3 us
    all_to_all x1, waiting for transfers between devices, local(): lax.all_to_all(outgoing.reshape(owners, capacity, BS * BS), ('row', 'col'...  28.4 us
    dot_general x2, matrix products, accumulate(): return jnp.dot(incoming, column_panel, preferred_element_type=jnp.float32)  25.1 us
    all_to_all x1, starting transfers between devices, local(): lax.all_to_all(labels.reshape(owners, capacity), ('row', 'col'), split_ax...  14.8 us
    transpose x1, local copies, waits for them, and re-layouts, local(): local_panel = collected.reshape(block_rows, block_cols, BS, BS).transpose...  14.2 us
  transfers between devices with their start and end apart: 6, of which 6 were waited for; matrix products, arithmetic and copies ran while one was open for 2% of the time, Pallas kernels for 0%

commit v1 on v0

--- a/solution.py
+++ b/solution.py
@@ -7,6 +7,14 @@
 BS = 32
 NBLK = 256
 COUPLING = 2.5
+
+
+def find_lines_up(block_here, comm_axis):
+    stack_in = []
+    for _ in range(lax.axis_size(comm_axis)):
+        stack_in.append(block_here)
+    reached = jnp.concatenate(lax.all_to_all(jnp.stack(stack_in), comm_axis, 0, 0), axis=0)
+    return reached
 
 
 def local(basis_left, basis_right, grid_weight, task_owner, task_block, core_matrix, block_mask):
@@ -84,7 +92,7 @@
     pattern_own = own_columns(pattern)
     identity_own = own_columns(identity)
     initial = (pattern_own * (0.5 * identity_own - coupling_scale * ks_out)).astype(jnp.bfloat16)
-    column_panel = lax.all_gather(initial, "row", axis=0, tiled=True)
+    column_panel = find_lines_up(initial, "row")
 
     def accumulate(incoming):
         return jnp.dot(incoming, column_panel, preferred_element_type=jnp.float32)

time: 536 us -> 514 us (0.959)
  waiting for transfers between devices: 422 us -> 342 us
  blocking collectives: 0 us -> 56.1 us
    all_to_all x0 -> x1, blocking collectives: none -> 56.1 us  [find_lines_up(): lax.all_to_all(jnp.stack(stack_in), comm_axis, 0, 0)]
    all_gather x1 -> x0, waiting for transfers between devices: 53.9 us -> none  [local(): column_panel = lax.all_gather(initial, 'row', axis=0, tiled=True)]
    all_gather x1, waiting for transfers between devices: 155 us -> 129 us  [local(): lax.all_gather(initial, ('col', 'layer'), axis=1, tiled=True)]
  transfers between devices with their start and end apart: 6 -> 5, of which waited for: 6 -> 5; matrix products, arithmetic and copies ran while one was open for 2% -> 3% of each run, Pallas kernels for 0% -> 0%
where the time goes in v1:
time: 514 us; the launch traced here: 513 us
  waiting for transfers between devices  342 us (67%)
  blocking collectives  56.1 us (11%)
  local copies, waits for them, and re-layouts  40.9 us (8%)
  matrix products  26.6 us (5%)
  starting transfers between devices  23.3 us (5%)
  between operations  14 us (3%)
  other arithmetic  10.4 us (2%)
    all_gather x1, waiting for transfers between devices, local(): lax.all_gather(square.astype(jnp.bfloat16), ('col', 'layer'), axis=1, til...  149 us
    all_gather x1, waiting for transfers between devices, local(): lax.all_gather(initial, ('col', 'layer'), axis=1, tiled=True)  129 us
    all_to_all x1, blocking collectives, find_lines_up(): lax.all_to_all(jnp.stack(stack_in), comm_axis, 0, 0)  56.1 us
    reduce_scatter x1, waiting for transfers between devices, local(): lax.psum_scatter(local_panel, 'layer', scatter_dimension=1, tiled=True)  30.3 us
    all_to_all x1, waiting for transfers between devices, local(): lax.all_to_all(outgoing.reshape(owners, capacity, BS * BS), ('row', 'col'...  28.4 us
    dot_general x2, matrix products, accumulate(): return jnp.dot(incoming, column_panel, preferred_element_type=jnp.float32)  24.8 us
    all_to_all x1, starting transfers between devices, local(): lax.all_to_all(labels.reshape(owners, capacity), ('row', 'col'), split_ax...  14.8 us
    transpose x1, local copies, waits for them, and re-layouts, local(): local_panel = collected.reshape(block_rows, block_cols, BS, BS).transpose...  14.2 us
  transfers between devices with their start and end apart: 5, of which 5 were waited for; matrix products, arithmetic and copies ran while one was open for 3% of the time, Pallas kernels for 0%

profile of v1, /device:TPU:1, one launch (start us, length us, event | category | flops | bytes accessed | tf_op | source)
XLA Modules:
  0.0 512.9 jit_solution(7955135764376656257)
XLA Ops:
  10.3 1.0 scatter_custom_fusion
  12.1 14.8 %all-to-all-start = ((f32[128,1,2]{2,1,0:T(1,128)}), f32[128,1,2]{2,1,0:T(1,128)S(1)}, u32[]{:S(2)}, u32[]{:S(2)}) async-start(f32[128,1,2]{2,1,0:T(1,128)} %bitcast.4), calls=%async_computation | async-start | bytes 131072 | tf_op jit(solution)/shard_map/all_to_all | solution.py:58
  26.9 1.9 fusion.2
  28.8 1.3 copy.22
  30.3 1.3 scatter_custom_fusion.1
  31.5 1.6 reshape.89
  33.1 4.3 all-to-all-done
  37.4 8.1 %all-to-all-start.1 = ((f32[128,2,1024]{2,1,0:T(2,128)}), f32[128,2,1024]{2,1,0:T(2,128)S(1)}, u32[]{:S(2)}, u32[]{:S(2)}) async-start(f32[128,2,1024]{2,1,0:T(2,128)} %reshape.89), calls=%async_computation.1 | async-start | bytes 2097152 | tf_op jit(solution)/shard_map/all_to_all | solution.py:51
  46.0 28.4 %all-to-all-done.1 = f32[128,2,1024]{2,1,0:T(2,128)S(1)} async-done(((f32[128,2,1024]{2,1,0:T(2,128)}), f32[128,2,1024]{2,1,0:T(2,128)S(1)}, u32[]{:S(2)}, u32[]{:S(2)}) %all-to-all-start.1) | async-done | bytes 1048608 | tf_op jit(solution)/shard_map/all_to_all | solution.py:51
  74.4 1.7 reshape.115
  76.1 4.0 scatter_custom_fusion.2
  80.1 4.8 reshape.91
  84.9 14.2 %copy.24 = f32[32,32,16,32]{3,2,1,0:T(8,128)} copy(f32[32,32,16,32]{3,1,2,0:T(8,128)} %bitcast.37) | data formatting | bytes 4194304 | tf_op jit(solution)/shard_map/transpose | solution.py:73
  99.0 7.3 %reshape.92 = f32[1024,512]{1,0:T(8,128)} reshape(f32[32,32,16,32]{3,2,1,0:T(8,128)} %copy.24) | data formatting | bytes 4194304 | tf_op jit(solution)/shard_map/reshape | solution.py:74
  107.4 1.3 copy.25
  108.7 2.6 reshape.87
  112.2 30.3 %reduce-scatter.2.cloned.1.call-done = f32[1024,256]{1,0:T(8,128)} async-done(((f32[1024,512]{1,0:T(8,128)}), f32[1024,256]{1,0:T(8,128)}) %reduce-scatter.2.cloned.1.call-update) | async-done | bytes 1048592 | tf_op jit(solution)/shard_map/reduce_scatter | solution.py:90
  142.5 3.0 fusion.5
  145.6 1.3 stack.2
  146.9 56.1 %all_to_all.19 = bf16[8,1024,256]{2,1,0:T(8,128)(2,1)} all-to-all(bf16[8,1024,256]{2,1,0:T(8,128)(2,1)S(1)} %stack.2), channel_id=1, replica_groups=mesh['row'=8,'col'=16,'layer'=2] {'row'}, dimensions={0} | all-to-all | bytes 8388608 | tf_op jit(solution)/shard_map/all_to_all | solution.py:16
  203.0 129.4 %all-gather.3.cloned.1.call-done = bf16[1024,8192]{1,0:T(8,128)(2,1)} async-done(((bf16[1024,256]{1,0:T(8,128)(2,1)}), bf16[1024,8192]{1,0:T(8,128)(2,1)}) %all-gather.3.cloned.1.call-update) | async-done | bytes 16777232 | tf_op jit(solution)/shard_map/all_gather | solution.py:100
  332.4 12.2 %fusion.16 = (bf16[1024,256]{1,0:T(8,128)(2,1)}, f32[1024,256]{1,0:T(8,128)S(1)}) fusion(bf16[1024,8192]{1,0:T(8,128)(2,1)} %all-gather.3.cloned.1.call-done, bf16[8192,256]{1,0:T(8,128)(2,1)} %bitcast.39, f32[1024,1,256]{2,0,1:T(8,128)S(1)} %copy-done.2), kind=kOutput, calls=%fused_computation.37 | convolution fusion | flops 4295491584 | bytes 23592960 | tf_op jit(solution)/shard_map/dot_general | solution.py:98
  344.7 149.2 %all-gather.5.cloned.1.call-done = bf16[1024,8192]{1,0:T(8,128)(2,1)} async-done(((bf16[1024,256]{1,0:T(8,128)(2,1)}), bf16[1024,8192]{1,0:T(8,128)(2,1)}) %all-gather.5.cloned.1.call-update) | async-done | bytes 16777232 | tf_op jit(solution)/shard_map/all_gather | solution.py:102
  493.9 12.5 %fusion.1 = f32[1024,256]{1,0:T(8,128)} fusion(bf16[1024,8192]{1,0:T(8,128)(2,1)} %all-gather.5.cloned.1.call-done, bf16[8192,256]{1,0:T(8,128)(2,1)} %bitcast.40, f32[1024,1,256]{2,0,1:T(8,128)S(1)} %copy-done.2, f32[1024,256]{1,0:T(8,128)S(1)} %get-tuple-element.5), kind=kOutput, calls=%fused_computation.7 | convolution fusion | flops 4296015872 | bytes 24117248 | tf_op jit(solution)/shard_map/dot_general | solution.py:98
  (35 shorter events, 6.5 us)
Async XLA Ops:
  7.2 19.7 %copy-start = (bf16[128,32,128]{2,1,0:T(8,128)(2,1)S(1)}, bf16[128,32,128]{2,1,0:T(8,128)(2,1)}, u32[]{:S(2)}) copy-start(bf16[128,32,128]{2,1,0:T(8,128)(2,1)} %param.8) | copy-start | bytes 3145732
  12.1 25.4 %all-to-all-start = ((f32[128,1,2]{2,1,0:T(1,128)}), f32[128,1,2]{2,1,0:T(1,128)S(1)}, u32[]{:S(2)}, u32[]{:S(2)}) async-start(f32[128,1,2]{2,1,0:T(1,128)} %bitcast.4), calls=%async_computation | async-start | bytes 131072 | tf_op jit(solution)/shard_map/all_to_all | solution.py:58
  37.4 36.9 %all-to-all-start.1 = ((f32[128,2,1024]{2,1,0:T(2,128)}), f32[128,2,1024]{2,1,0:T(2,128)S(1)}, u32[]{:S(2)}, u32[]{:S(2)}) async-start(f32[128,2,1024]{2,1,0:T(2,128)} %reshape.89), calls=%async_computation.1 | async-start | bytes 2097152 | tf_op jit(solution)/shard_map/all_to_all | solution.py:51
  45.6 96.9 %reduce-scatter.2.cloned.1.call-start = ((), (), s32[]{:S(2)}) async-start(), calls=%async_computation.4 | async-start | bytes 3145728 | tf_op jit(solution)/shard_map/reduce_scatter | solution.py:90
  99.0 7.7 %copy-start.3 = (s32[32,16]{0,1:T(8,128)S(1)}, s32[32,16]{0,1:T(8,128)}, u32[]{:S(2)}) copy-start(s32[32,16]{0,1:T(8,128)} %param.13) | copy-start | bytes 6148
  106.4 226.0 %all-gather.3.cloned.1.call-start = ((), (), s32[]{:S(2)}) async-start(), calls=%async_computation.5 | async-start | bytes 17301504 | tf_op jit(solution)/shard_map/all_gather | solution.py:100
  145.5 348.4 %all-gather.5.cloned.1.call-start = ((), (), s32[]{:S(2)}) async-start(), calls=%async_computation.6 | async-start | bytes 17301504 | tf_op jit(solution)/shard_map/all_gather | solution.py:102
  146.9 185.5 %copy-start.2 = (f32[1024,1,256]{2,0,1:T(8,128)S(1)}, f32[1024,1,256]{2,0,1:T(8,128)}, u32[]{:S(2)}) copy-start(f32[1024,1,256]{2,0,1:T(8,128)} %copy.25) | copy-start | bytes 3145732
  493.9 12.5 %copy-start.1 = (bf16[128,32,128]{2,1,0:T(8,128)(2,1)S(1)}, bf16[128,32,128]{2,1,0:T(8,128)(2,1)}, u32[]{:S(2)}) copy-start(bf16[128,32,128]{2,1,0:T(8,128)(2,1)} %param.8) | copy-start | bytes 3145732
Sparse Core Ops, SparseCore 0:
  106.5 35.9 reduce-scatter.1
  145.6 186.7 all-gather.2
  344.8 149.0 all-gather.4
